TPU v7x, 32 devices: a whole 2x2x4 slice. The times are simulated.
32 devices in a mesh: vel: 16 (over z, x, core), gx: 2 (over y).
Axes of the slice: x: 2, y: 2, z: 4, core: 2. Of those that a mesh axis runs over, the one named last changes fastest.
Arguments:
- distribution: float32 [4096, 8, 256], P('vel', 'gx'), as said below
Outputs:
- relaxed: float32 [4096, 8, 256], P('vel', 'gx')
Inputs may be any that keep to these rules, and one draw needn't show every extreme that they name: `distribution`: every entry is positive.
All inputs are finite; a program needn't handle non-finite values.
Results may differ from a plain program's by a relative error of at most 0.0003.
Values sent between devices are 32-bit elements; how exact they have to be, the bound alone decides.
A program may use at most 64 MiB of HBM per device.

v0:
```python
import math
import jax
import jax.numpy as jnp
from jax import lax
from jax.sharding import PartitionSpec as P

NV1 = 16
NZ = 16
COLLISIONS = 2
speed_limit = 4.0
time_step = 0.05
knudsen = 0.0125


def extended(value, sides, width):
    for axis, dim in sides:
        size, length = (lax.axis_size(axis), value.shape[dim])
        up = [(i, (i + 1) % size) for i in range(size)]
        down = [(j, i) for i, j in up]
        last = lax.slice_in_dim(value, length - width, length, axis=dim)
        leading = lax.slice_in_dim(value, 0, width, axis=dim)
        before = lax.ppermute(last, axis, up)
        after = lax.ppermute(leading, axis, down)
        value = jnp.concatenate([before, value, after], axis=dim)
    return value


def velocities(index):
    spacing = 2.0 * speed_limit / (NV1 - 1)
    first = index % NV1
    rest = index // NV1
    second = rest // NV1
    third = rest % NV1
    return [-speed_limit + spacing * part.astype(jnp.float32) for part in (first, second, third)]


def quad_weight():
    spacing = 2.0 * speed_limit / (NV1 - 1)
    return spacing**3 / (2.0 * math.pi) ** 1.5


def along_z(field, offset):
    zpos = jnp.arange(field.shape[-1], dtype=jnp.int32) % NZ
    main = jnp.roll(field, offset, -1)
    if offset > 0:
        other = jnp.roll(field, offset - NZ, -1)
        keep = zpos >= offset
    else:
        other = jnp.roll(field, offset + NZ, -1)
        keep = zpos < NZ + offset
    return jnp.where(keep, main, other)


def backward(field, minus_one, minus_two):
    return (3.0 * field - 4.0 * minus_one + minus_two) * 0.5


def forward(field, plus_one, plus_two):
    return (-3.0 * field + 4.0 * plus_one - plus_two) * 0.5


def upwind(field, comp, minus_one, minus_two, plus_one, plus_two):
    return jnp.where(
        comp > 0, backward(field, minus_one, minus_two), forward(field, plus_one, plus_two)
    )


def transverse(field, comp_y, comp_z):
    deriv_y = upwind(
        field,
        comp_y,
        jnp.roll(field, NZ, -1),
        jnp.roll(field, 2 * NZ, -1),
        jnp.roll(field, -NZ, -1),
        jnp.roll(field, -2 * NZ, -1),
    )
    deriv_z = upwind(
        field, comp_z, along_z(field, 1), along_z(field, 2), along_z(field, -1), along_z(field, -2)
    )
    return (deriv_y, deriv_z)


def along_x(field, comp_x):
    padded = extended(field, (("gx", 1),), 2)
    return upwind(field, comp_x, padded[:, 1:-3], padded[:, :-4], padded[:, 3:-1], padded[:, 4:])


def rate(field, comp_x, comp_y, comp_z):
    deriv_x = along_x(field, comp_x)
    deriv_y, deriv_z = transverse(field, comp_y, comp_z)
    return -(comp_x * deriv_x + comp_y * deriv_y + comp_z * deriv_z)


def advance(field, comp_x, comp_y, comp_z):
    first = field + time_step * rate(field, comp_x, comp_y, comp_z)
    second = 0.75 * field + 0.25 * (first + time_step * rate(first, comp_x, comp_y, comp_z))
    return field / 3.0 + 2.0 / 3.0 * (second + time_step * rate(second, comp_x, comp_y, comp_z))


def primitive(moments):
    rho = moments[0]
    vel_x = moments[1] / rho
    vel_y = moments[2] / rho
    vel_z = moments[3] / rho
    temp = (moments[4] / rho - (vel_x * vel_x + vel_y * vel_y + vel_z * vel_z)) / 3.0
    return jnp.stack([rho, vel_x, vel_y, vel_z, temp])


def maxwell(prims, comp_x, comp_y, comp_z):
    spread = (comp_x - prims[1]) ** 2 + (comp_y - prims[2]) ** 2 + (comp_z - prims[3]) ** 2
    return prims[0] * prims[4] ** (-1.5) * jnp.exp(-spread / (2.0 * prims[4]))


def separable_mass(prims):
    spacing = 2.0 * speed_limit / (NV1 - 1)
    points = -speed_limit + spacing * jnp.arange(NV1, dtype=jnp.float32)
    product = quad_weight() * prims[0] * prims[4] ** (-1.5)
    for which in (1, 2, 3):
        offset = points[:, None] - prims[which][None, :]
        product = product * jnp.sum(jnp.exp(-(offset * offset) / (2.0 * prims[4])), 0)
    return product


def collide(field, comp_x, comp_y, comp_z):
    count = field.shape[0]
    flat = field.reshape(count, -1)
    ones = jnp.ones_like(comp_x)
    table = (
        jnp.stack(
            [ones, comp_x, comp_y, comp_z, comp_x * comp_x + comp_y * comp_y + comp_z * comp_z]
        )
        * quad_weight()
    )
    local = jnp.dot(table, flat, precision=lax.Precision.HIGHEST)
    prims = primitive(lax.psum(local, "vel"))
    dense = maxwell(prims, comp_x[:, None], comp_y[:, None], comp_z[:, None])
    mass = separable_mass(prims)
    scale = prims[0] / mass
    rates = time_step * prims[0] * jnp.sqrt(prims[4]) / knudsen
    return ((flat + rates * (dense * scale)) / (1.0 + rates)).reshape(field.shape)


def on_device(distribution):
    count = distribution.shape[0]
    index = lax.axis_index("vel") * count + jnp.arange(count, dtype=jnp.int32)
    comp_x, comp_y, comp_z = velocities(index)
    field = distribution
    for step in range(COLLISIONS):
        field = advance(field, comp_x[:, None, None], comp_y[:, None, None], comp_z[:, None, None])
        field = collide(field, comp_x, comp_y, comp_z)
    return field


def solution(mesh):
    return jax.shard_map(
        on_device,
        mesh=mesh,
        in_specs=(P("vel", "gx", None),),
        out_specs=P("vel", "gx", None),
        check_vma=False,
    )
```

profile of v0, /device:TPU:0, one launch (start us, length us, event | category | flops | bytes accessed | tf_op | source)
XLA Modules:
  0.0 386.0 jit_solution(4824331936601160539)
XLA Ops:
  0.0 2.1 fusion.320
  2.9 3.0 collective-permute-start.1
  13.6 1.5 fusion.316
  15.1 1.5 fusion.318
  16.5 1.5 fusion.313
  18.0 1.5 fusion.309
  21.3 1.5 fusion.310
  22.8 2.1 copy.101
  24.8 4.6 %collective-permute-done = f32[256,2,256]{2,0,1:T(8,128)} collective-permute-done((f32[256,2,256]{2,0,1:T(8,128)}, f32[256,2,256]{2,0,1:T(8,128)}, u32[]{:S(2)}, u32[]{:S(2)}) %collective-permute-start) | collective-permute-done | bytes 524320 | tf_op jit(solution)/shard_map/ppermute | solution.py:22
  29.4 2.0 copy.96
  31.4 7.4 %fusion.104 = f32[256,4,256]{0,2,1:T(8,128)S(1)} fusion(f32[256,4,256]{0,2,1:T(8,128)S(1)} %copy.92, f32[256,2,256]{0,2,1:T(8,128)} %copy.101, f32[256,2,256]{0,2,1:T(8,128)} %copy.96, f32[256,4,240]{0,2,1:T(8,128)} %get-tuple-element.188, f32[256,4,16]{0,2,1:T(8,128)S(1)} %get-tuple-element.190, f32[256,4,224]{0,2,1:T(8,128)} %get-tuple-element.184, ...), kind=kLoop, calls=%fused_computation.128 | loop fusion | flops 14942208 | bytes 15733504 | tf_op jit(solution)/shard_map/add | solution.py:95
  40.9 1.4 fusion.303
  42.3 1.5 fusion.305
  43.8 1.5 fusion.300
  45.3 1.4 fusion.296
  46.7 1.5 fusion.301
  50.2 1.7 collective-permute-start.3
  52.8 1.5 fusion.297
  54.3 11.0 %collective-permute-done.3 = f32[256,2,256]{2,0,1:T(8,128)} collective-permute-done((f32[256,2,256]{2,0,1:T(8,128)}, f32[256,2,256]{2,0,1:T(8,128)}, u32[]{:S(2)}, u32[]{:S(2)}) %collective-permute-start.3) | collective-permute-done | bytes 524320 | tf_op jit(solution)/shard_map/ppermute | solution.py:23
  65.3 2.0 copy.130
  67.4 7.4 %collective-permute-done.2 = f32[256,2,256]{2,0,1:T(8,128)S(1)} collective-permute-done((f32[256,2,256]{2,0,1:T(8,128)S(1)}, f32[256,2,256]{2,0,1:T(8,128)S(1)}, u32[]{:S(2)}, u32[]{:S(2)}) %collective-permute-start.2) | collective-permute-done | bytes 524320 | tf_op jit(solution)/shard_map/ppermute | solution.py:22
  75.7 7.5 %fusion.87 = f32[256,4,256]{0,2,1:T(8,128)S(1)} fusion(f32[256,4,256]{0,2,1:T(8,128)S(1)} %fusion.104, f32[256,2,256]{0,2,1:T(8,128)} %copy.130, f32[256,2,256]{0,2,1:T(8,128)} %copy.128, f32[256,4,240]{0,2,1:T(8,128)} %get-tuple-element.162, f32[256,4,16]{0,2,1:T(8,128)S(1)} %get-tuple-element.164, f32[256,4,224]{0,2,1:T(8,128)} %get-tuple-element.158, ...), kind=kLoop, calls=%fused_computation.111 | loop fusion | flops 15728640 | bytes 16782080 | tf_op jit(solution)/shard_map/add | solution.py:96
  85.3 1.4 fusion.290
  86.7 1.5 fusion.292
  88.2 1.5 fusion.287
  89.7 1.4 fusion.283
  91.1 1.5 fusion.288
  94.6 1.5 collective-permute-start.5
  97.2 1.5 fusion.284
  98.7 11.0 %collective-permute-done.5 = f32[256,2,256]{2,0,1:T(8,128)} collective-permute-done((f32[256,2,256]{2,0,1:T(8,128)}, f32[256,2,256]{2,0,1:T(8,128)}, u32[]{:S(2)}, u32[]{:S(2)}) %collective-permute-start.5) | collective-permute-done | bytes 524320 | tf_op jit(solution)/shard_map/ppermute | solution.py:23
  109.7 2.0 copy.134
  111.8 6.5 %collective-permute-done.4 = f32[256,2,256]{2,0,1:T(8,128)S(1)} collective-permute-done((f32[256,2,256]{2,0,1:T(8,128)S(1)}, f32[256,2,256]{2,0,1:T(8,128)S(1)}, u32[]{:S(2)}, u32[]{:S(2)}) %collective-permute-start.4) | collective-permute-done | bytes 524320 | tf_op jit(solution)/shard_map/ppermute | solution.py:22
  119.3 7.5 %fusion.68 = f32[256,4,256]{0,2,1:T(8,128)S(1)} fusion(f32[256,4,256]{0,2,1:T(8,128)S(1)} %fusion.87, f32[256,2,256]{0,2,1:T(8,128)} %copy.134, f32[256,2,256]{0,2,1:T(8,128)} %copy.132, f32[256,4,240]{0,2,1:T(8,128)} %get-tuple-element.136, f32[256,4,16]{0,2,1:T(8,128)S(1)} %get-tuple-element.138, f32[256,4,224]{0,2,1:T(8,128)} %get-tuple-element.132, ...), kind=kLoop, calls=%fused_computation.92 | loop fusion | flops 15728640 | bytes 16782080 | tf_op jit(solution)/shard_map/add | solution.py:97
  127.8 58.6 %psum.14 = f32[5,1024]{1,0:T(8,128)S(1)} all-reduce(f32[5,1024]{1,0:T(8,128)S(1)} %fusion.208), channel_id=1, replica_groups=mesh['vel'=16,'gx'=2] {'vel'}, use_global_device_ids=true, to_apply=%region_0.1 | all-reduce | flops 5120 | bytes 40960 | tf_op jit(solution)/shard_map/psum | solution.py:135
  193.4 1.5 fusion.279
  195.0 1.5 fusion.274
  196.4 1.4 fusion.270
  197.9 1.5 fusion.275
  201.4 1.5 collective-permute-start.7
  204.0 1.5 fusion.271
  205.4 11.0 %collective-permute-done.7 = f32[256,2,256]{2,0,1:T(8,128)} collective-permute-done((f32[256,2,256]{2,0,1:T(8,128)}, f32[256,2,256]{2,0,1:T(8,128)}, u32[]{:S(2)}, u32[]{:S(2)}) %collective-permute-start.7) | collective-permute-done | bytes 524320 | tf_op jit(solution)/shard_map/ppermute | solution.py:23
  216.5 2.0 copy.138
  218.5 3.6 collective-permute-done.6
  223.1 7.3 %fusion.49 = f32[256,4,256]{0,2,1:T(8,128)S(1)} fusion(f32[256,4,256]{0,2,1:T(8,128)S(1)} %add_divide_fusion.1, f32[256,2,256]{0,2,1:T(8,128)} %copy.138, f32[256,2,256]{0,2,1:T(8,128)} %copy.136, f32[256,4,240]{0,2,1:T(8,128)} %get-tuple-element.110, f32[256,4,16]{0,2,1:T(8,128)S(1)} %get-tuple-element.112, f32[256,4,224]{0,2,1:T(8,128)} %get-tuple-element.106, ...), kind=kLoop, calls=%fused_computation.73 | loop fusion | flops 14942208 | bytes 15733504 | tf_op jit(solution)/shard_map/add | solution.py:95
  234.0 1.5 fusion.266
  235.5 1.5 fusion.261
  237.0 1.4 fusion.257
  238.4 1.5 fusion.262
  241.9 1.5 collective-permute-start.9
  244.5 1.5 fusion.258
  246.0 10.3 %collective-permute-done.9 = f32[256,2,256]{2,0,1:T(8,128)} collective-permute-done((f32[256,2,256]{2,0,1:T(8,128)}, f32[256,2,256]{2,0,1:T(8,128)}, u32[]{:S(2)}, u32[]{:S(2)}) %collective-permute-start.9) | collective-permute-done | bytes 524320 | tf_op jit(solution)/shard_map/ppermute | solution.py:23
  256.3 2.0 copy.142
  258.3 3.5 collective-permute-done.8
  262.8 8.2 %fusion.32 = f32[256,4,256]{0,2,1:T(8,128)S(1)} fusion(f32[256,4,256]{0,2,1:T(8,128)S(1)} %fusion.49, f32[256,2,256]{0,2,1:T(8,128)} %copy.142, f32[256,2,256]{0,2,1:T(8,128)} %copy.140, f32[256,4,240]{0,2,1:T(8,128)} %get-tuple-element.84, f32[256,4,16]{0,2,1:T(8,128)S(1)} %get-tuple-element.86, f32[256,4,224]{0,2,1:T(8,128)} %get-tuple-element.80, ...), kind=kLoop, calls=%fused_computation.56 | loop fusion | flops 19660800 | bytes 16814848 | tf_op jit(solution)/shard_map/add | solution.py:96
  274.5 1.5 fusion.253
  276.0 1.5 fusion.248
  278.9 1.5 fusion.249
  282.4 1.5 collective-permute-start.11
  285.0 1.5 fusion.245
  286.5 9.5 %collective-permute-done.11 = f32[256,2,256]{2,0,1:T(8,128)} collective-permute-done((f32[256,2,256]{2,0,1:T(8,128)}, f32[256,2,256]{2,0,1:T(8,128)}, u32[]{:S(2)}, u32[]{:S(2)}) %collective-permute-start.11) | collective-permute-done | bytes 524320 | tf_op jit(solution)/shard_map/ppermute | solution.py:23
  296.0 2.0 copy.146
  298.0 3.5 collective-permute-done.10
  302.5 8.4 %fusion.13 = f32[256,4,256]{0,2,1:T(8,128)S(1)} fusion(f32[256,4,256]{0,2,1:T(8,128)S(1)} %fusion.32, f32[256,2,256]{0,2,1:T(8,128)} %copy.146, f32[256,2,256]{0,2,1:T(8,128)} %copy.144, f32[256,4,240]{0,2,1:T(8,128)} %get-tuple-element.58, f32[256,4,16]{0,2,1:T(8,128)S(1)} %get-tuple-element.60, f32[256,4,224]{0,2,1:T(8,128)} %get-tuple-element.54, ...), kind=kLoop, calls=%fused_computation.37 | loop fusion | flops 19660800 | bytes 16814848 | tf_op jit(solution)/shard_map/add | solution.py:97
  311.9 69.8 %psum.15 = f32[5,1024]{1,0:T(8,128)S(1)} all-reduce(f32[5,1024]{1,0:T(8,128)S(1)} %fusion.206), channel_id=1, replica_groups=mesh['vel'=16,'gx'=2] {'vel'}, use_global_device_ids=true, to_apply=%region_4.5 | all-reduce | flops 5120 | bytes 40960 | tf_op jit(solution)/shard_map/psum | solution.py:135
  (158 shorter events, 56.3 us)
Async XLA Ops:
  2.1 9.2 %copy-start = (f32[256,4,256]{2,1,0:T(4,128)S(1)}, f32[256,4,256]{2,1,0:T(4,128)}, u32[]{:S(2)}) copy-start(f32[256,4,256]{2,1,0:T(4,128)} %param.1) | copy-start | bytes 3145732
  2.9 19.9 %collective-permute-start.1 = (f32[256,2,256]{2,0,1:T(8,128)}, f32[256,2,256]{2,0,1:T(8,128)}, u32[]{:S(2)}, u32[]{:S(2)}) collective-permute-start(f32[256,2,256]{2,0,1:T(8,128)} %copy.149), channel_id=1, source_target_pairs={{1,0},{0,1},{3,2},{2,3},{5,4},{4,5},{7,6},{6,7},{9,8},{8,9},{11,10... | collective-permute-start | bytes 1572872 | tf_op jit(solution)/shard_map/ppermute | solution.py:23
  6.7 22.6 %collective-permute-start = (f32[256,2,256]{2,0,1:T(8,128)}, f32[256,2,256]{2,0,1:T(8,128)}, u32[]{:S(2)}, u32[]{:S(2)}) collective-permute-start(f32[256,2,256]{2,0,1:T(8,128)} %copy.148), channel_id=1, source_target_pairs={{0,1},{1,0},{2,3},{3,2},{4,5},{5,4},{6,7},{7,6},{8,9},{9,8},{10,11... | collective-permute-start | bytes 1572872 | tf_op jit(solution)/shard_map/ppermute | solution.py:22
  19.5 1.1 copy-start.16
  19.5 1.1 copy-start.17
  19.5 1.1 copy-start.18
  19.5 1.1 copy-start.19
  49.2 2.7 copy-start.1
  50.2 15.1 %collective-permute-start.3 = (f32[256,2,256]{2,0,1:T(8,128)}, f32[256,2,256]{2,0,1:T(8,128)}, u32[]{:S(2)}, u32[]{:S(2)}) collective-permute-start(f32[256,2,256]{2,0,1:T(8,128)} %copy.129), channel_id=1, source_target_pairs={{1,0},{0,1},{3,2},{2,3},{5,4},{4,5},{7,6},{6,7},{9,8},{8,9},{11,10... | collective-permute-start | bytes 1572872 | tf_op jit(solution)/shard_map/ppermute | solution.py:23
  51.9 22.8 %collective-permute-start.2 = (f32[256,2,256]{2,0,1:T(8,128)S(1)}, f32[256,2,256]{2,0,1:T(8,128)S(1)}, u32[]{:S(2)}, u32[]{:S(2)}) collective-permute-start(f32[256,2,256]{2,0,1:T(8,128)S(1)} %copy-done.1), channel_id=1, source_target_pairs={{0,1},{1,0},{2,3},{3,2},{4,5},{5,4},{6,7},{7,6},{8,9},{9,8},{10,11... | collective-permute-start | bytes 1572872 | tf_op jit(solution)/shard_map/ppermute | solution.py:22
  93.6 2.5 copy-start.2
  94.6 15.1 %collective-permute-start.5 = (f32[256,2,256]{2,0,1:T(8,128)}, f32[256,2,256]{2,0,1:T(8,128)}, u32[]{:S(2)}, u32[]{:S(2)}) collective-permute-start(f32[256,2,256]{2,0,1:T(8,128)} %copy.133), channel_id=1, source_target_pairs={{1,0},{0,1},{3,2},{2,3},{5,4},{4,5},{7,6},{6,7},{9,8},{8,9},{11,10... | collective-permute-start | bytes 1572872 | tf_op jit(solution)/shard_map/ppermute | solution.py:23
  96.1 22.2 %collective-permute-start.4 = (f32[256,2,256]{2,0,1:T(8,128)S(1)}, f32[256,2,256]{2,0,1:T(8,128)S(1)}, u32[]{:S(2)}, u32[]{:S(2)}) collective-permute-start(f32[256,2,256]{2,0,1:T(8,128)S(1)} %copy-done.2), channel_id=1, source_target_pairs={{0,1},{1,0},{2,3},{3,2},{4,5},{5,4},{6,7},{7,6},{8,9},{9,8},{10,11... | collective-permute-start | bytes 1572872 | tf_op jit(solution)/shard_map/ppermute | solution.py:22
  126.8 60.8 %copy-start.20 = (f32[16]{0:T(128)S(1)}, f32[16]{0:T(128)}, u32[]{:S(2)}) copy-start(f32[16]{0:T(128)} %multiply_add_fusion.9) | copy-start | bytes 196
  126.8 61.8 %copy-start.6 = (f32[256]{0:T(256)S(1)}, f32[256]{0:T(256)}, u32[]{:S(2)}) copy-start(f32[256]{0:T(256)} %fusion.228) | copy-start | bytes 3076
  187.5 2.3 copy-start.8
  187.5 2.3 copy-start.9
  187.6 2.3 copy-start.10
  187.8 2.1 copy-start.11
  187.9 2.0 copy-start.12
  187.9 2.0 copy-start.13
  188.5 1.4 copy-start.14
  188.6 1.4 copy-start.15
  200.4 2.5 copy-start.3
  201.4 15.1 %collective-permute-start.7 = (f32[256,2,256]{2,0,1:T(8,128)}, f32[256,2,256]{2,0,1:T(8,128)}, u32[]{:S(2)}, u32[]{:S(2)}) collective-permute-start(f32[256,2,256]{2,0,1:T(8,128)} %copy.137), channel_id=1, source_target_pairs={{1,0},{0,1},{3,2},{2,3},{5,4},{4,5},{7,6},{6,7},{9,8},{8,9},{11,10... | collective-permute-start | bytes 1572872 | tf_op jit(solution)/shard_map/ppermute | solution.py:23
  202.9 19.2 %collective-permute-start.6 = (f32[256,2,256]{2,0,1:T(8,128)S(1)}, f32[256,2,256]{2,0,1:T(8,128)S(1)}, u32[]{:S(2)}, u32[]{:S(2)}) collective-permute-start(f32[256,2,256]{2,0,1:T(8,128)S(1)} %copy-done.3), channel_id=1, source_target_pairs={{0,1},{1,0},{2,3},{3,2},{4,5},{5,4},{6,7},{7,6},{8,9},{9,8},{10,11... | collective-permute-start | bytes 1572872 | tf_op jit(solution)/shard_map/ppermute | solution.py:22
  240.9 2.5 copy-start.4
  241.9 14.4 %collective-permute-start.9 = (f32[256,2,256]{2,0,1:T(8,128)}, f32[256,2,256]{2,0,1:T(8,128)}, u32[]{:S(2)}, u32[]{:S(2)}) collective-permute-start(f32[256,2,256]{2,0,1:T(8,128)} %copy.141), channel_id=1, source_target_pairs={{1,0},{0,1},{3,2},{2,3},{5,4},{4,5},{7,6},{6,7},{9,8},{8,9},{11,10... | collective-permute-start | bytes 1572872 | tf_op jit(solution)/shard_map/ppermute | solution.py:23
  243.4 18.4 %collective-permute-start.8 = (f32[256,2,256]{2,0,1:T(8,128)S(1)}, f32[256,2,256]{2,0,1:T(8,128)S(1)}, u32[]{:S(2)}, u32[]{:S(2)}) collective-permute-start(f32[256,2,256]{2,0,1:T(8,128)S(1)} %copy-done.4), channel_id=1, source_target_pairs={{0,1},{1,0},{2,3},{3,2},{4,5},{5,4},{6,7},{7,6},{8,9},{9,8},{10,11... | collective-permute-start | bytes 1572872 | tf_op jit(solution)/shard_map/ppermute | solution.py:22
  281.4 2.5 copy-start.5
  282.4 13.6 %collective-permute-start.11 = (f32[256,2,256]{2,0,1:T(8,128)}, f32[256,2,256]{2,0,1:T(8,128)}, u32[]{:S(2)}, u32[]{:S(2)}) collective-permute-start(f32[256,2,256]{2,0,1:T(8,128)} %copy.145), channel_id=1, source_target_pairs={{1,0},{0,1},{3,2},{2,3},{5,4},{4,5},{7,6},{6,7},{9,8},{8,9},{11,10... | collective-permute-start | bytes 1572872 | tf_op jit(solution)/shard_map/ppermute | solution.py:23
  283.9 17.6 %collective-permute-start.10 = (f32[256,2,256]{2,0,1:T(8,128)S(1)}, f32[256,2,256]{2,0,1:T(8,128)S(1)}, u32[]{:S(2)}, u32[]{:S(2)}) collective-permute-start(f32[256,2,256]{2,0,1:T(8,128)S(1)} %copy-done.5), channel_id=1, source_target_pairs={{0,1},{1,0},{2,3},{3,2},{4,5},{5,4},{6,7},{7,6},{8,9},{9,8},{10,11... | collective-permute-start | bytes 1572872 | tf_op jit(solution)/shard_map/ppermute | solution.py:22
  311.0 71.5 %copy-start.21 = (f32[16]{0:T(128)S(1)}, f32[16]{0:T(128)}, u32[]{:S(2)}) copy-start(f32[16]{0:T(128)} %multiply_add_fusion.9) | copy-start | bytes 196
  311.0 72.4 %copy-start.7 = (f32[256]{0:T(256)S(1)}, f32[256]{0:T(256)}, u32[]{:S(2)}) copy-start(f32[256]{0:T(256)} %fusion.228) | copy-start | bytes 3076
where the time goes:
time: 387 us; the launch traced here: 386 us
  blocking collectives  128 us (33%)
  local copies, waits for them, and re-layouts  104 us (27%)
  waiting for transfers between devices  81.9 us (21%)
  other arithmetic  56.3 us (15%)
  starting transfers between devices  13.1 us (3%)
    psum x2, blocking collectives, collide(): prims = primitive(lax.psum(local, 'vel'))  128 us
    ppermute x6, waiting for transfers between devices, extended(): after = lax.ppermute(leading, axis, down)  52.9 us
    ppermute x6, waiting for transfers between devices, extended(): before = lax.ppermute(last, axis, up)  29 us
    slice x24, local copies, waits for them, and re-layouts, along_z(): other = jnp.roll(field, offset + NZ, -1)  25.4 us
    slice x24, local copies, waits for them, and re-layouts, along_z(): main = jnp.roll(field, offset, -1)  24.6 us
    add x2, other arithmetic, advance(): field / 3.0  15.9 us
    add x2, other arithmetic, advance(): 0.75 * field  15.6 us
    add x2, other arithmetic, advance(): first = field + time_step * rate(field, comp_x, comp_y, comp_z)  14.7 us
  transfers between devices with their start and end apart: 12, of which 11 were waited for; matrix products, arithmetic and copies ran while one was open for 10% of the time, Pallas kernels for 0%

commit v1 on v0

--- a/solution.py
+++ b/solution.py
@@ -132,7 +132,7 @@
         * quad_weight()
     )
     local = jnp.dot(table, flat, precision=lax.Precision.HIGHEST)
-    prims = primitive(lax.psum(local, "vel"))
+    prims = primitive(jnp.sum(lax.all_gather(local, "vel"), axis=0))
     dense = maxwell(prims, comp_x[:, None], comp_y[:, None], comp_z[:, None])
     mass = separable_mass(prims)
     scale = prims[0] / mass

time: 387 us -> 315 us (0.81)
  blocking collectives: 128 us -> 41.9 us
  waiting for transfers between devices: 81.9 us -> 96.4 us
    psum x2 -> x0, blocking collectives: 128 us -> none  [collide(): prims = primitive(lax.psum(local, 'vel'))]
    all_gather x0 -> x2, blocking collectives: none -> 41.9 us  [collide(): prims = primitive(jnp.sum(lax.all_gather(local, 'vel'), axis=0))]
    ppermute x6, waiting for transfers between devices: 29 us -> 41.3 us  [extended(): before = lax.ppermute(last, axis, up)]
  transfers between devices with their start and end apart: 12 -> 12, of which waited for: 11 -> 11; matrix products, arithmetic and copies ran while one was open for 10% -> 13% of each run, Pallas kernels for 0% -> 0%
where the time goes in v1:
time: 315 us; the launch traced here: 314 us
  local copies, waits for them, and re-layouts  104 us (33%)
  waiting for transfers between devices  96.4 us (31%)
  other arithmetic  56.4 us (18%)
  blocking collectives  41.9 us (13%)
  starting transfers between devices  13.1 us (4%)
    ppermute x6, waiting for transfers between devices, extended(): after = lax.ppermute(leading, axis, down)  55.1 us
    all_gather x2, blocking collectives, collide(): prims = primitive(jnp.sum(lax.all_gather(local, 'vel'), axis=0))  41.9 us
    ppermute x6, waiting for transfers between devices, extended(): before = lax.ppermute(last, axis, up)  41.3 us
    slice x24, local copies, waits for them, and re-layouts, along_z(): other = jnp.roll(field, offset + NZ, -1)  25.4 us
    slice x24, local copies, waits for them, and re-layouts, along_z(): main = jnp.roll(field, offset, -1)  24.6 us
    add x2, other arithmetic, advance(): field / 3.0  15.9 us
    add x2, other arithmetic, advance(): 0.75 * field  15.6 us
    add x2, other arithmetic, advance(): first = field + time_step * rate(field, comp_x, comp_y, comp_z)  14.7 us
  transfers between devices with their start and end apart: 12, of which 11 were waited for; matrix products, arithmetic and copies ran while one was open for 13% of the time, Pallas kernels for 0%

profile of v1, /device:TPU:0, one launch (start us, length us, event | category | flops | bytes accessed | tf_op | source)
XLA Modules:
  0.0 314.1 jit_solution(1132410315355761608)
XLA Ops:
  0.0 2.1 fusion.318
  2.9 3.0 collective-permute-start.1
  13.6 1.5 fusion.314
  15.1 1.5 fusion.316
  16.5 1.5 fusion.311
  18.0 1.5 fusion.307
  21.3 1.5 fusion.308
  22.8 2.1 copy.101
  24.8 4.6 %collective-permute-done = f32[256,2,256]{2,0,1:T(8,128)} collective-permute-done((f32[256,2,256]{2,0,1:T(8,128)}, f32[256,2,256]{2,0,1:T(8,128)}, u32[]{:S(2)}, u32[]{:S(2)}) %collective-permute-start) | collective-permute-done | bytes 524320 | tf_op jit(solution)/shard_map/ppermute | solution.py:22
  29.4 2.0 copy.96
  31.4 7.4 %fusion.104 = f32[256,4,256]{0,2,1:T(8,128)S(1)} fusion(f32[256,4,256]{0,2,1:T(8,128)S(1)} %copy.92, f32[256,2,256]{0,2,1:T(8,128)} %copy.101, f32[256,2,256]{0,2,1:T(8,128)} %copy.96, f32[256,4,240]{0,2,1:T(8,128)} %get-tuple-element.188, f32[256,4,16]{0,2,1:T(8,128)S(1)} %get-tuple-element.190, f32[256,4,224]{0,2,1:T(8,128)} %get-tuple-element.184, ...), kind=kLoop, calls=%fused_computation.130 | loop fusion | flops 14942208 | bytes 15733504 | tf_op jit(solution)/shard_map/add | solution.py:95
  40.9 1.4 fusion.301
  42.3 1.5 fusion.303
  43.8 1.5 fusion.298
  45.3 1.4 fusion.294
  46.7 1.5 fusion.299
  50.2 1.7 collective-permute-start.3
  52.8 1.5 fusion.295
  54.3 11.0 %collective-permute-done.3 = f32[256,2,256]{2,0,1:T(8,128)} collective-permute-done((f32[256,2,256]{2,0,1:T(8,128)}, f32[256,2,256]{2,0,1:T(8,128)}, u32[]{:S(2)}, u32[]{:S(2)}) %collective-permute-start.3) | collective-permute-done | bytes 524320 | tf_op jit(solution)/shard_map/ppermute | solution.py:23
  65.3 2.0 copy.130
  67.4 7.4 %collective-permute-done.2 = f32[256,2,256]{2,0,1:T(8,128)S(1)} collective-permute-done((f32[256,2,256]{2,0,1:T(8,128)S(1)}, f32[256,2,256]{2,0,1:T(8,128)S(1)}, u32[]{:S(2)}, u32[]{:S(2)}) %collective-permute-start.2) | collective-permute-done | bytes 524320 | tf_op jit(solution)/shard_map/ppermute | solution.py:22
  75.7 7.5 %fusion.87 = f32[256,4,256]{0,2,1:T(8,128)S(1)} fusion(f32[256,4,256]{0,2,1:T(8,128)S(1)} %fusion.104, f32[256,2,256]{0,2,1:T(8,128)} %copy.130, f32[256,2,256]{0,2,1:T(8,128)} %copy.128, f32[256,4,240]{0,2,1:T(8,128)} %get-tuple-element.162, f32[256,4,16]{0,2,1:T(8,128)S(1)} %get-tuple-element.164, f32[256,4,224]{0,2,1:T(8,128)} %get-tuple-element.158, ...), kind=kLoop, calls=%fused_computation.113 | loop fusion | flops 15728640 | bytes 16782080 | tf_op jit(solution)/shard_map/add | solution.py:96
  85.3 1.4 fusion.288
  86.7 1.5 fusion.290
  88.2 1.5 fusion.285
  89.7 1.4 fusion.281
  91.1 1.5 fusion.286
  94.6 1.5 collective-permute-start.5
  97.2 1.5 fusion.282
  98.7 11.0 %collective-permute-done.5 = f32[256,2,256]{2,0,1:T(8,128)} collective-permute-done((f32[256,2,256]{2,0,1:T(8,128)}, f32[256,2,256]{2,0,1:T(8,128)}, u32[]{:S(2)}, u32[]{:S(2)}) %collective-permute-start.5) | collective-permute-done | bytes 524320 | tf_op jit(solution)/shard_map/ppermute | solution.py:23
  109.7 2.0 copy.134
  111.8 6.5 %collective-permute-done.4 = f32[256,2,256]{2,0,1:T(8,128)S(1)} collective-permute-done((f32[256,2,256]{2,0,1:T(8,128)S(1)}, f32[256,2,256]{2,0,1:T(8,128)S(1)}, u32[]{:S(2)}, u32[]{:S(2)}) %collective-permute-start.4) | collective-permute-done | bytes 524320 | tf_op jit(solution)/shard_map/ppermute | solution.py:22
  119.3 7.5 %fusion.68 = f32[256,4,256]{0,2,1:T(8,128)S(1)} fusion(f32[256,4,256]{0,2,1:T(8,128)S(1)} %fusion.87, f32[256,2,256]{0,2,1:T(8,128)} %copy.134, f32[256,2,256]{0,2,1:T(8,128)} %copy.132, f32[256,4,240]{0,2,1:T(8,128)} %get-tuple-element.136, f32[256,4,16]{0,2,1:T(8,128)S(1)} %get-tuple-element.138, f32[256,4,224]{0,2,1:T(8,128)} %get-tuple-element.132, ...), kind=kLoop, calls=%fused_computation.94 | loop fusion | flops 15728640 | bytes 16782080 | tf_op jit(solution)/shard_map/add | solution.py:97
  127.8 23.1 %all-gather.2 = f32[16,5,1024]{2,1,0:T(8,128)S(1)} all-gather(f32[1,5,1024]{2,1,0:T(8,128)S(1)} %convolution_bitcast_fusion.1), channel_id=2, replica_groups=mesh['vel'=16,'gx'=2] {'vel'}, dimensions={0}, use_global_device_ids=true | all-gather | bytes 348160 | tf_op jit(solution)/shard_map/all_gather | solution.py:135
  158.1 1.5 fusion.277
  159.6 1.5 fusion.272
  161.1 1.4 fusion.268
  162.5 1.5 fusion.273
  166.0 1.5 collective-permute-start.7
  168.6 1.5 fusion.269
  170.1 11.0 %collective-permute-done.7 = f32[256,2,256]{2,0,1:T(8,128)} collective-permute-done((f32[256,2,256]{2,0,1:T(8,128)}, f32[256,2,256]{2,0,1:T(8,128)}, u32[]{:S(2)}, u32[]{:S(2)}) %collective-permute-start.7) | collective-permute-done | bytes 524320 | tf_op jit(solution)/shard_map/ppermute | solution.py:23
  181.1 2.0 copy.138
  183.1 8.5 %collective-permute-done.6 = f32[256,2,256]{2,0,1:T(8,128)S(1)} collective-permute-done((f32[256,2,256]{2,0,1:T(8,128)S(1)}, f32[256,2,256]{2,0,1:T(8,128)S(1)}, u32[]{:S(2)}, u32[]{:S(2)}) %collective-permute-start.6) | collective-permute-done | bytes 524320 | tf_op jit(solution)/shard_map/ppermute | solution.py:22
  192.6 7.3 %fusion.49 = f32[256,4,256]{0,2,1:T(8,128)S(1)} fusion(f32[256,4,256]{0,2,1:T(8,128)S(1)} %add_divide_fusion.1, f32[256,2,256]{0,2,1:T(8,128)} %copy.138, f32[256,2,256]{0,2,1:T(8,128)} %copy.136, f32[256,4,240]{0,2,1:T(8,128)} %get-tuple-element.110, f32[256,4,16]{0,2,1:T(8,128)S(1)} %get-tuple-element.112, f32[256,4,224]{0,2,1:T(8,128)} %get-tuple-element.106, ...), kind=kLoop, calls=%fused_computation.75 | loop fusion | flops 14942208 | bytes 15733504 | tf_op jit(solution)/shard_map/add | solution.py:95
  203.5 1.5 fusion.264
  205.0 1.5 fusion.259
  206.5 1.4 fusion.255
  207.9 1.5 fusion.260
  211.4 1.5 collective-permute-start.9
  214.0 1.5 fusion.256
  215.5 11.0 %collective-permute-done.9 = f32[256,2,256]{2,0,1:T(8,128)} collective-permute-done((f32[256,2,256]{2,0,1:T(8,128)}, f32[256,2,256]{2,0,1:T(8,128)}, u32[]{:S(2)}, u32[]{:S(2)}) %collective-permute-start.9) | collective-permute-done | bytes 524320 | tf_op jit(solution)/shard_map/ppermute | solution.py:23
  226.5 2.0 copy.142
  228.5 7.6 %collective-permute-done.8 = f32[256,2,256]{2,0,1:T(8,128)S(1)} collective-permute-done((f32[256,2,256]{2,0,1:T(8,128)S(1)}, f32[256,2,256]{2,0,1:T(8,128)S(1)}, u32[]{:S(2)}, u32[]{:S(2)}) %collective-permute-start.8) | collective-permute-done | bytes 524320 | tf_op jit(solution)/shard_map/ppermute | solution.py:22
  237.1 8.2 %fusion.32 = f32[256,4,256]{0,2,1:T(8,128)S(1)} fusion(f32[256,4,256]{0,2,1:T(8,128)S(1)} %fusion.49, f32[256,2,256]{0,2,1:T(8,128)} %copy.142, f32[256,2,256]{0,2,1:T(8,128)} %copy.140, f32[256,4,240]{0,2,1:T(8,128)} %get-tuple-element.84, f32[256,4,16]{0,2,1:T(8,128)S(1)} %get-tuple-element.86, f32[256,4,224]{0,2,1:T(8,128)} %get-tuple-element.80, ...), kind=kLoop, calls=%fused_computation.58 | loop fusion | flops 19660800 | bytes 16814848 | tf_op jit(solution)/shard_map/add | solution.py:96
  248.8 1.5 fusion.251
  250.3 1.5 fusion.246
  253.2 1.5 fusion.247
  256.7 1.5 collective-permute-start.11
  259.4 1.5 fusion.243
  260.8 11.0 %collective-permute-done.11 = f32[256,2,256]{2,0,1:T(8,128)} collective-permute-done((f32[256,2,256]{2,0,1:T(8,128)}, f32[256,2,256]{2,0,1:T(8,128)}, u32[]{:S(2)}, u32[]{:S(2)}) %collective-permute-start.11) | collective-permute-done | bytes 524320 | tf_op jit(solution)/shard_map/ppermute | solution.py:23
  271.8 2.0 copy.146
  273.9 6.8 %collective-permute-done.10 = f32[256,2,256]{2,0,1:T(8,128)S(1)} collective-permute-done((f32[256,2,256]{2,0,1:T(8,128)S(1)}, f32[256,2,256]{2,0,1:T(8,128)S(1)}, u32[]{:S(2)}, u32[]{:S(2)}) %collective-permute-start.10) | collective-permute-done | bytes 524320 | tf_op jit(solution)/shard_map/ppermute | solution.py:22
  281.6 8.4 %fusion.13 = f32[256,4,256]{0,2,1:T(8,128)S(1)} fusion(f32[256,4,256]{0,2,1:T(8,128)S(1)} %fusion.32, f32[256,2,256]{0,2,1:T(8,128)} %copy.146, f32[256,2,256]{0,2,1:T(8,128)} %copy.144, f32[256,4,240]{0,2,1:T(8,128)} %get-tuple-element.58, f32[256,4,16]{0,2,1:T(8,128)S(1)} %get-tuple-element.60, f32[256,4,224]{0,2,1:T(8,128)} %get-tuple-element.54, ...), kind=kLoop, calls=%fused_computation.39 | loop fusion | flops 19660800 | bytes 16814848 | tf_op jit(solution)/shard_map/add | solution.py:97
  291.1 18.7 %all-gather.3 = f32[16,5,1024]{2,1,0:T(8,128)S(1)} all-gather(f32[1,5,1024]{2,1,0:T(8,128)S(1)} %convolution_bitcast_fusion), channel_id=3, replica_groups=mesh['vel'=16,'gx'=2] {'vel'}, dimensions={0}, use_global_device_ids=true | all-gather | bytes 348160 | tf_op jit(solution)/shard_map/all_gather | solution.py:135
  (160 shorter events, 56.4 us)
Async XLA Ops:
  2.1 9.2 %copy-start = (f32[256,4,256]{2,1,0:T(4,128)S(1)}, f32[256,4,256]{2,1,0:T(4,128)}, u32[]{:S(2)}) copy-start(f32[256,4,256]{2,1,0:T(4,128)} %param.1) | copy-start | bytes 3145732
  2.9 19.9 %collective-permute-start.1 = (f32[256,2,256]{2,0,1:T(8,128)}, f32[256,2,256]{2,0,1:T(8,128)}, u32[]{:S(2)}, u32[]{:S(2)}) collective-permute-start(f32[256,2,256]{2,0,1:T(8,128)} %copy.149), channel_id=1, source_target_pairs={{1,0},{0,1},{3,2},{2,3},{5,4},{4,5},{7,6},{6,7},{9,8},{8,9},{11,10... | collective-permute-start | bytes 1572872 | tf_op jit(solution)/shard_map/ppermute | solution.py:23
  6.7 22.6 %collective-permute-start = (f32[256,2,256]{2,0,1:T(8,128)}, f32[256,2,256]{2,0,1:T(8,128)}, u32[]{:S(2)}, u32[]{:S(2)}) collective-permute-start(f32[256,2,256]{2,0,1:T(8,128)} %copy.148), channel_id=1, source_target_pairs={{0,1},{1,0},{2,3},{3,2},{4,5},{5,4},{6,7},{7,6},{8,9},{9,8},{10,11... | collective-permute-start | bytes 1572872 | tf_op jit(solution)/shard_map/ppermute | solution.py:22
  19.5 1.1 copy-start.16
  19.5 1.1 copy-start.17
  19.5 1.1 copy-start.18
  19.5 1.1 copy-start.19
  49.2 2.7 copy-start.1
  50.2 15.1 %collective-permute-start.3 = (f32[256,2,256]{2,0,1:T(8,128)}, f32[256,2,256]{2,0,1:T(8,128)}, u32[]{:S(2)}, u32[]{:S(2)}) collective-permute-start(f32[256,2,256]{2,0,1:T(8,128)} %copy.129), channel_id=1, source_target_pairs={{1,0},{0,1},{3,2},{2,3},{5,4},{4,5},{7,6},{6,7},{9,8},{8,9},{11,10... | collective-permute-start | bytes 1572872 | tf_op jit(solution)/shard_map/ppermute | solution.py:23
  51.9 22.8 %collective-permute-start.2 = (f32[256,2,256]{2,0,1:T(8,128)S(1)}, f32[256,2,256]{2,0,1:T(8,128)S(1)}, u32[]{:S(2)}, u32[]{:S(2)}) collective-permute-start(f32[256,2,256]{2,0,1:T(8,128)S(1)} %copy-done.1), channel_id=1, source_target_pairs={{0,1},{1,0},{2,3},{3,2},{4,5},{5,4},{6,7},{7,6},{8,9},{9,8},{10,11... | collective-permute-start | bytes 1572872 | tf_op jit(solution)/shard_map/ppermute | solution.py:22
  93.6 2.5 copy-start.2
  94.6 15.1 %collective-permute-start.5 = (f32[256,2,256]{2,0,1:T(8,128)}, f32[256,2,256]{2,0,1:T(8,128)}, u32[]{:S(2)}, u32[]{:S(2)}) collective-permute-start(f32[256,2,256]{2,0,1:T(8,128)} %copy.133), channel_id=1, source_target_pairs={{1,0},{0,1},{3,2},{2,3},{5,4},{4,5},{7,6},{6,7},{9,8},{8,9},{11,10... | collective-permute-start | bytes 1572872 | tf_op jit(solution)/shard_map/ppermute | solution.py:23
  96.1 22.2 %collective-permute-start.4 = (f32[256,2,256]{2,0,1:T(8,128)S(1)}, f32[256,2,256]{2,0,1:T(8,128)S(1)}, u32[]{:S(2)}, u32[]{:S(2)}) collective-permute-start(f32[256,2,256]{2,0,1:T(8,128)S(1)} %copy-done.2), channel_id=1, source_target_pairs={{0,1},{1,0},{2,3},{3,2},{4,5},{5,4},{6,7},{7,6},{8,9},{9,8},{10,11... | collective-permute-start | bytes 1572872 | tf_op jit(solution)/shard_map/ppermute | solution.py:22
  126.8 25.5 %copy-start.20 = (f32[16]{0:T(128)S(1)}, f32[16]{0:T(128)}, u32[]{:S(2)}) copy-start(f32[16]{0:T(128)} %multiply_add_fusion.9) | copy-start | bytes 196
  126.8 26.4 %copy-start.6 = (f32[256]{0:T(256)S(1)}, f32[256]{0:T(256)}, u32[]{:S(2)}) copy-start(f32[256]{0:T(256)} %fusion.226) | copy-start | bytes 3076
  152.1 2.3 copy-start.8
  152.2 2.3 copy-start.9
  152.2 2.3 copy-start.10
  152.5 2.1 copy-start.11
  152.5 2.0 copy-start.12
  152.5 2.0 copy-start.13
  153.2 1.4 copy-start.14
  153.2 1.4 copy-start.15
  165.0 2.5 copy-start.3
  166.0 15.1 %collective-permute-start.7 = (f32[256,2,256]{2,0,1:T(8,128)}, f32[256,2,256]{2,0,1:T(8,128)}, u32[]{:S(2)}, u32[]{:S(2)}) collective-permute-start(f32[256,2,256]{2,0,1:T(8,128)} %copy.137), channel_id=1, source_target_pairs={{1,0},{0,1},{3,2},{2,3},{5,4},{4,5},{7,6},{6,7},{9,8},{8,9},{11,10... | collective-permute-start | bytes 1572872 | tf_op jit(solution)/shard_map/ppermute | solution.py:23
  167.5 24.1 %collective-permute-start.6 = (f32[256,2,256]{2,0,1:T(8,128)S(1)}, f32[256,2,256]{2,0,1:T(8,128)S(1)}, u32[]{:S(2)}, u32[]{:S(2)}) collective-permute-start(f32[256,2,256]{2,0,1:T(8,128)S(1)} %copy-done.3), channel_id=1, source_target_pairs={{0,1},{1,0},{2,3},{3,2},{4,5},{5,4},{6,7},{7,6},{8,9},{9,8},{10,11... | collective-permute-start | bytes 1572872 | tf_op jit(solution)/shard_map/ppermute | solution.py:22
  210.4 2.5 copy-start.4
  211.4 15.1 %collective-permute-start.9 = (f32[256,2,256]{2,0,1:T(8,128)}, f32[256,2,256]{2,0,1:T(8,128)}, u32[]{:S(2)}, u32[]{:S(2)}) collective-permute-start(f32[256,2,256]{2,0,1:T(8,128)} %copy.141), channel_id=1, source_target_pairs={{1,0},{0,1},{3,2},{2,3},{5,4},{4,5},{7,6},{6,7},{9,8},{8,9},{11,10... | collective-permute-start | bytes 1572872 | tf_op jit(solution)/shard_map/ppermute | solution.py:23
  212.9 23.2 %collective-permute-start.8 = (f32[256,2,256]{2,0,1:T(8,128)S(1)}, f32[256,2,256]{2,0,1:T(8,128)S(1)}, u32[]{:S(2)}, u32[]{:S(2)}) collective-permute-start(f32[256,2,256]{2,0,1:T(8,128)S(1)} %copy-done.4), channel_id=1, source_target_pairs={{0,1},{1,0},{2,3},{3,2},{4,5},{5,4},{6,7},{7,6},{8,9},{9,8},{10,11... | collective-permute-start | bytes 1572872 | tf_op jit(solution)/shard_map/ppermute | solution.py:22
  255.7 2.5 copy-start.5
  256.7 15.1 %collective-permute-start.11 = (f32[256,2,256]{2,0,1:T(8,128)}, f32[256,2,256]{2,0,1:T(8,128)}, u32[]{:S(2)}, u32[]{:S(2)}) collective-permute-start(f32[256,2,256]{2,0,1:T(8,128)} %copy.145), channel_id=1, source_target_pairs={{1,0},{0,1},{3,2},{2,3},{5,4},{4,5},{7,6},{6,7},{9,8},{8,9},{11,10... | collective-permute-start | bytes 1572872 | tf_op jit(solution)/shard_map/ppermute | solution.py:23
  258.2 22.4 %collective-permute-start.10 = (f32[256,2,256]{2,0,1:T(8,128)S(1)}, f32[256,2,256]{2,0,1:T(8,128)S(1)}, u32[]{:S(2)}, u32[]{:S(2)}) collective-permute-start(f32[256,2,256]{2,0,1:T(8,128)S(1)} %copy-done.5), channel_id=1, source_target_pairs={{0,1},{1,0},{2,3},{3,2},{4,5},{5,4},{6,7},{7,6},{8,9},{9,8},{10,11... | collective-permute-start | bytes 1572872 | tf_op jit(solution)/shard_map/ppermute | solution.py:22
  290.1 20.5 %copy-start.21 = (f32[16]{0:T(128)S(1)}, f32[16]{0:T(128)}, u32[]{:S(2)}) copy-start(f32[16]{0:T(128)} %multiply_add_fusion.9) | copy-start | bytes 196
  290.1 21.4 %copy-start.7 = (f32[256]{0:T(256)S(1)}, f32[256]{0:T(256)}, u32[]{:S(2)}) copy-start(f32[256]{0:T(256)} %fusion.226) | copy-start | bytes 3076
